TPU v7x, 512 devices: a whole 4x8x8 slice. The times are simulated.
512 devices in a mesh: tok: 64 (over y, z), head: 8 (over x, core).
Axes of the slice: x: 4, y: 8, z: 8, core: 2. Of those that a mesh axis runs over, the one named last changes fastest.
Arguments:
- query_rows: bfloat16 [32768, 4096], P('tok', 'head'), may hold values from -8 to 8
- key_rows: bfloat16 [32768, 1024], P('tok', 'head'), may hold values from -8 to 8
- value_rows: bfloat16 [32768, 1024], P('tok', 'head'), may hold values from -12 to 12
- out_weight: bfloat16 [4096, 4096], P(None, 'head'), may hold values from -0.09375 to 0.09375
- doc_lengths: int32 [32], replicated, may hold values from 1 to 8192, 32768 in all
Outputs:
- mixed: bfloat16 [32768, 4096], P('tok', 'head')
Inputs may be any that keep to these rules, and one draw needn't show every extreme that they name: `doc_lengths`: the lengths sum to 32768 and the longest document has exactly 8192 tokens.
All inputs are finite; a program needn't handle non-finite values.
Results may differ from a plain program's by a relative error of at most 0.0053.
Values may be sent and summed in bfloat16 or wider, within the bound.
No kernel may reach another device: no remote copies, remote signals or barrier semaphores. Data moves between devices by JAX's collectives and lax.ppermute only.
A program may use at most 64 MiB of HBM per device.

v0:
```python
import math

import jax
import jax.numpy as jnp
from jax import lax
from jax.sharding import PartitionSpec as P

QHEADS = 32
KVH = 8
HD = 128
TILE = 128
KB = 512


very_negative = -1e30


def from_behind(value, axis, steps):
    count = lax.axis_size(axis)
    leading, last = (max(0, -steps), min(count, count - steps))
    return lax.ppermute(value, axis, [(source, source + steps) for source in range(leading, last)])


def document_start(positions, doc_lengths):
    doc_ends = jnp.cumsum(doc_lengths)
    doc_starts = doc_ends - doc_lengths
    inside = (positions[:, None] >= doc_starts[None, :]) & (positions[:, None] < doc_ends[None, :])
    return jnp.sum(jnp.where(inside, doc_starts[None, :], 0), axis=1)


def attend_tile(query_tile, tile_first, key_win, value_win, win_start, doc_lengths):
    tile_rows = query_tile.shape[0]
    kv_local = key_win.shape[1] // HD
    group_size = QHEADS // KVH
    window_len = key_win.shape[0]
    score_scale = 1.0 / math.sqrt(HD)
    row_pos = tile_first + jnp.arange(tile_rows, dtype=jnp.int32)
    doc_start = document_start(row_pos, doc_lengths)
    queries = query_tile.reshape(tile_rows, kv_local, group_size, HD).transpose(1, 2, 0, 3)
    queries = queries.reshape(kv_local, group_size * tile_rows, HD)
    stacked_pos = jnp.tile(row_pos, group_size)
    stacked_start = jnp.tile(doc_start, group_size)
    first_local = doc_start[0] - win_start
    turn_count = (tile_first + tile_rows - doc_start[0] + KB - 1) // KB
    keys_split = key_win.reshape(window_len, kv_local, HD)
    values_split = value_win.reshape(window_len, kv_local, HD)

    def attend_block(which_block, carried):
        running_max, denominator, accumulated = carried
        fresh_from = first_local + which_block * KB
        offset = jnp.minimum(fresh_from, window_len - KB)
        key_block = lax.dynamic_slice_in_dim(keys_split, offset, KB, 0)
        value_block = lax.dynamic_slice_in_dim(values_split, offset, KB, 0)
        local_idx = offset + jnp.arange(KB, dtype=jnp.int32)
        key_pos = win_start + local_idx
        allowed = (
            (local_idx[None, :] >= fresh_from)
            & (key_pos[None, :] >= stacked_start[:, None])
            & (key_pos[None, :] <= stacked_pos[:, None])
        )
        scores = (
            jnp.einsum("crd,kcd->crk", queries, key_block, preferred_element_type=jnp.float32)
            * score_scale
        )
        scores = jnp.where(allowed[None], scores, very_negative)
        new_max = jnp.maximum(running_max, jnp.max(scores, axis=2))
        exponent = jnp.where(allowed[None], jnp.exp(scores - new_max[:, :, None]), 0.0)
        rescale = jnp.exp(running_max - new_max)
        denominator = denominator * rescale + jnp.sum(exponent, axis=2)
        weights = exponent.astype(jnp.bfloat16)
        accumulated = accumulated * rescale[:, :, None] + jnp.einsum(
            "crk,kcd->crd", weights, value_block, preferred_element_type=jnp.float32
        )
        return (new_max, denominator, accumulated)

    start_max = jnp.full((kv_local, group_size * tile_rows), very_negative, jnp.float32)
    start_sum = jnp.zeros((kv_local, group_size * tile_rows), jnp.float32)
    start_acc = jnp.zeros((kv_local, group_size * tile_rows, HD), jnp.float32)
    running_max, denominator, accumulated = lax.fori_loop(
        0, turn_count, attend_block, (start_max, start_sum, start_acc)
    )
    safe_sum = jnp.where(denominator > 0.0, denominator, 1.0)
    output = accumulated / safe_sum[:, :, None]
    output = output.reshape(kv_local, group_size, tile_rows, HD).transpose(2, 0, 1, 3)
    return output.reshape(tile_rows, kv_local * group_size * HD).astype(jnp.bfloat16)


def fetch_earlier(key_rows, value_rows, distance):
    return from_behind((key_rows, value_rows), "tok", distance)


def local(query_rows, key_rows, value_rows, out_weight, doc_lengths):
    tok_count = lax.axis_size("tok")
    tok_index = lax.axis_index("tok")
    tok_dev = query_rows.shape[0]
    q_width = query_rows.shape[1]
    per_device = tok_dev // TILE
    span_devices = min(32, tok_count // 4)
    earlier_pieces = [
        fetch_earlier(key_rows, value_rows, distance) for distance in range(span_devices, 0, -1)
    ]
    all_pieces = earlier_pieces + [(key_rows, value_rows)]
    key_win = jnp.concatenate([piece[0] for piece in all_pieces], axis=0)
    value_win = jnp.concatenate([piece[1] for piece in all_pieces], axis=0)
    win_start = (tok_index - span_devices) * tok_dev

    def run_slot(slot_args):
        query_tile, tile_first = slot_args
        return attend_tile(query_tile, tile_first, key_win, value_win, win_start, doc_lengths)

    tile_starts = tok_index * tok_dev + jnp.arange(per_device, dtype=jnp.int32) * TILE
    results = lax.map(run_slot, (query_rows.reshape(per_device, TILE, q_width), tile_starts))
    attended = results.reshape(tok_dev, q_width)
    summed = jnp.dot(
        lax.all_gather(attended, "head", axis=1, tiled=True),
        out_weight,
        preferred_element_type=jnp.float32,
    )
    return summed.astype(jnp.bfloat16)


def solution(mesh):
    return jax.shard_map(
        local,
        mesh=mesh,
        in_specs=(P("tok", "head"), P("tok", "head"), P("tok", "head"), P(None, "head"), P()),
        out_specs=P("tok", "head"),
        check_vma=False,
    )
```

profile of v0, /device:TPU:1, one launch (start us, length us, event | category | flops | bytes accessed | tf_op | source)
XLA Modules:
  0.0 414.8 jit_solution(17227242606668043142)
XLA Ops:
  6.5 5.2 %collective-permute-start = (bf16[512,128]{1,0:T(8,128)(2,1)}, bf16[512,128]{1,0:T(8,128)(2,1)S(1)}, u32[]{:S(2)}, u32[]{:S(2)}) collective-permute-start(bf16[512,128]{1,0:T(8,128)(2,1)} %param.10), channel_id=1, source_target_pairs={{0,128},{8,136},{16,144},{24,152},{32,160},{40,168},{48,176},{56,1... | collective-permute-start | bytes 393224 | tf_op jit(solution)/shard_map/ppermute | solution.py:21
  11.7 11.7 %collective-permute-start.1 = (bf16[512,128]{1,0:T(8,128)(2,1)}, bf16[512,128]{1,0:T(8,128)(2,1)S(1)}, u32[]{:S(2)}, u32[]{:S(2)}) collective-permute-start(bf16[512,128]{1,0:T(8,128)(2,1)} %param.10), channel_id=1, source_target_pairs={{0,120},{8,128},{16,136},{24,144},{32,152},{40,160},{48,168},{56,1... | collective-permute-start | bytes 393224 | tf_op jit(solution)/shard_map/ppermute | solution.py:21
  23.4 4.5 %collective-permute-start.2 = (bf16[512,128]{1,0:T(8,128)(2,1)}, bf16[512,128]{1,0:T(8,128)(2,1)S(1)}, u32[]{:S(2)}, u32[]{:S(2)}) collective-permute-start(bf16[512,128]{1,0:T(8,128)(2,1)} %param.10), channel_id=1, source_target_pairs={{0,112},{8,120},{16,128},{24,136},{32,144},{40,152},{48,160},{56,1... | collective-permute-start | bytes 393224 | tf_op jit(solution)/shard_map/ppermute | solution.py:21
  27.9 1.3 collective-permute-start.3
  29.2 7.8 %collective-permute-start.4 = (bf16[512,128]{1,0:T(8,128)(2,1)}, bf16[512,128]{1,0:T(8,128)(2,1)S(1)}, u32[]{:S(2)}, u32[]{:S(2)}) collective-permute-start(bf16[512,128]{1,0:T(8,128)(2,1)} %param.10), channel_id=1, source_target_pairs={{0,96},{8,104},{16,112},{24,120},{32,128},{40,136},{48,144},{56,15... | collective-permute-start | bytes 393224 | tf_op jit(solution)/shard_map/ppermute | solution.py:21
  38.7 1.3 collective-permute-start.5
  40.0 3.8 collective-permute-start.6
  43.9 1.3 collective-permute-start.7
  45.2 1.8 collective-permute-start.8
  47.1 7.2 %collective-permute-start.9 = (bf16[512,128]{1,0:T(8,128)(2,1)}, bf16[512,128]{1,0:T(8,128)(2,1)S(1)}, u32[]{:S(2)}, u32[]{:S(2)}) collective-permute-start(bf16[512,128]{1,0:T(8,128)(2,1)} %param.10), channel_id=1, source_target_pairs={{0,56},{8,64},{16,72},{24,80},{32,88},{40,96},{48,104},{56,112},{6... | collective-permute-start | bytes 393224 | tf_op jit(solution)/shard_map/ppermute | solution.py:21
  54.4 3.0 collective-permute-start.10
  57.4 6.7 %collective-permute-start.11 = (bf16[512,128]{1,0:T(8,128)(2,1)}, bf16[512,128]{1,0:T(8,128)(2,1)S(1)}, u32[]{:S(2)}, u32[]{:S(2)}) collective-permute-start(bf16[512,128]{1,0:T(8,128)(2,1)} %param.10), channel_id=1, source_target_pairs={{0,40},{8,48},{16,56},{24,64},{32,72},{40,80},{48,88},{56,96},{64,... | collective-permute-start | bytes 393224 | tf_op jit(solution)/shard_map/ppermute | solution.py:21
  64.2 10.9 %collective-permute-start.12 = (bf16[512,128]{1,0:T(8,128)(2,1)}, bf16[512,128]{1,0:T(8,128)(2,1)S(1)}, u32[]{:S(2)}, u32[]{:S(2)}) collective-permute-start(bf16[512,128]{1,0:T(8,128)(2,1)} %param.10), channel_id=1, source_target_pairs={{0,32},{8,40},{16,48},{24,56},{32,64},{40,72},{48,80},{56,88},{64,... | collective-permute-start | bytes 393224 | tf_op jit(solution)/shard_map/ppermute | solution.py:21
  75.2 1.8 collective-permute-start.13
  77.1 6.5 %collective-permute-start.14 = (bf16[512,128]{1,0:T(8,128)(2,1)S(1)}, bf16[512,128]{1,0:T(8,128)(2,1)S(1)}, u32[]{:S(2)}, u32[]{:S(2)}) collective-permute-start(bf16[512,128]{1,0:T(8,128)(2,1)S(1)} %copy-done.1), channel_id=1, source_target_pairs={{0,16},{8,24},{16,32},{24,40},{32,48},{40,56},{48,64},{56,72},{64,... | collective-permute-start | bytes 393224 | tf_op jit(solution)/shard_map/ppermute | solution.py:21
  83.6 3.5 collective-permute-start.15
  87.2 5.1 %collective-permute-start.16 = (bf16[512,128]{1,0:T(8,128)(2,1)S(1)}, bf16[512,128]{1,0:T(8,128)(2,1)S(1)}, u32[]{:S(2)}, u32[]{:S(2)}) collective-permute-start(bf16[512,128]{1,0:T(8,128)(2,1)S(1)} %copy-done.2), channel_id=1, source_target_pairs={{0,128},{8,136},{16,144},{24,152},{32,160},{40,168},{48,176},{56,1... | collective-permute-start | bytes 393224 | tf_op jit(solution)/shard_map/ppermute | solution.py:21
  92.4 5.4 %collective-permute-start.17 = (bf16[512,128]{1,0:T(8,128)(2,1)S(1)}, bf16[512,128]{1,0:T(8,128)(2,1)S(1)}, u32[]{:S(2)}, u32[]{:S(2)}) collective-permute-start(bf16[512,128]{1,0:T(8,128)(2,1)S(1)} %copy-done.2), channel_id=1, source_target_pairs={{0,120},{8,128},{16,136},{24,144},{32,152},{40,160},{48,168},{56,1... | collective-permute-start | bytes 393224 | tf_op jit(solution)/shard_map/ppermute | solution.py:21
  97.9 5.2 %collective-permute-start.18 = (bf16[512,128]{1,0:T(8,128)(2,1)S(1)}, bf16[512,128]{1,0:T(8,128)(2,1)S(1)}, u32[]{:S(2)}, u32[]{:S(2)}) collective-permute-start(bf16[512,128]{1,0:T(8,128)(2,1)S(1)} %copy-done.2), channel_id=1, source_target_pairs={{0,112},{8,120},{16,128},{24,136},{32,144},{40,152},{48,160},{56,1... | collective-permute-start | bytes 393224 | tf_op jit(solution)/shard_map/ppermute | solution.py:21
  103.1 7.0 %collective-permute-start.19 = (bf16[512,128]{1,0:T(8,128)(2,1)S(1)}, bf16[512,128]{1,0:T(8,128)(2,1)S(1)}, u32[]{:S(2)}, u32[]{:S(2)}) collective-permute-start(bf16[512,128]{1,0:T(8,128)(2,1)S(1)} %copy-done.2), channel_id=1, source_target_pairs={{0,104},{8,112},{16,120},{24,128},{32,136},{40,144},{48,152},{56,1... | collective-permute-start | bytes 393224 | tf_op jit(solution)/shard_map/ppermute | solution.py:21
  110.2 6.8 %collective-permute-start.20 = (bf16[512,128]{1,0:T(8,128)(2,1)S(1)}, bf16[512,128]{1,0:T(8,128)(2,1)S(1)}, u32[]{:S(2)}, u32[]{:S(2)}) collective-permute-start(bf16[512,128]{1,0:T(8,128)(2,1)S(1)} %copy-done.2), channel_id=1, source_target_pairs={{0,96},{8,104},{16,112},{24,120},{32,128},{40,136},{48,144},{56,15... | collective-permute-start | bytes 393224 | tf_op jit(solution)/shard_map/ppermute | solution.py:21
  117.1 2.0 collective-permute-start.21
  119.1 4.2 %collective-permute-start.22 = (bf16[512,128]{1,0:T(8,128)(2,1)S(1)}, bf16[512,128]{1,0:T(8,128)(2,1)S(1)}, u32[]{:S(2)}, u32[]{:S(2)}) collective-permute-start(bf16[512,128]{1,0:T(8,128)(2,1)S(1)} %copy-done.2), channel_id=1, source_target_pairs={{0,80},{8,88},{16,96},{24,104},{32,112},{40,120},{48,128},{56,136}... | collective-permute-start | bytes 393224 | tf_op jit(solution)/shard_map/ppermute | solution.py:21
  123.3 1.8 collective-permute-start.23
  125.2 4.3 %collective-permute-start.24 = (bf16[512,128]{1,0:T(8,128)(2,1)S(1)}, bf16[512,128]{1,0:T(8,128)(2,1)S(1)}, u32[]{:S(2)}, u32[]{:S(2)}) collective-permute-start(bf16[512,128]{1,0:T(8,128)(2,1)S(1)} %copy-done.2), channel_id=1, source_target_pairs={{0,64},{8,72},{16,80},{24,88},{32,96},{40,104},{48,112},{56,120},{... | collective-permute-start | bytes 393224 | tf_op jit(solution)/shard_map/ppermute | solution.py:21
  129.5 9.5 %collective-permute-start.25 = (bf16[512,128]{1,0:T(8,128)(2,1)S(1)}, bf16[512,128]{1,0:T(8,128)(2,1)S(1)}, u32[]{:S(2)}, u32[]{:S(2)}) collective-permute-start(bf16[512,128]{1,0:T(8,128)(2,1)S(1)} %copy-done.2), channel_id=1, source_target_pairs={{0,56},{8,64},{16,72},{24,80},{32,88},{40,96},{48,104},{56,112},{6... | collective-permute-start | bytes 393224 | tf_op jit(solution)/shard_map/ppermute | solution.py:21
  139.0 1.4 collective-permute-start.26
  140.4 6.7 %collective-permute-start.27 = (bf16[512,128]{1,0:T(8,128)(2,1)S(1)}, bf16[512,128]{1,0:T(8,128)(2,1)S(1)}, u32[]{:S(2)}, u32[]{:S(2)}) collective-permute-start(bf16[512,128]{1,0:T(8,128)(2,1)S(1)} %copy-done.2), channel_id=1, source_target_pairs={{0,40},{8,48},{16,56},{24,64},{32,72},{40,80},{48,88},{56,96},{64,... | collective-permute-start | bytes 393224 | tf_op jit(solution)/shard_map/ppermute | solution.py:21
  147.1 6.6 %collective-permute-start.28 = (bf16[512,128]{1,0:T(8,128)(2,1)S(1)}, bf16[512,128]{1,0:T(8,128)(2,1)S(1)}, u32[]{:S(2)}, u32[]{:S(2)}) collective-permute-start(bf16[512,128]{1,0:T(8,128)(2,1)S(1)} %copy-done.2), channel_id=1, source_target_pairs={{0,32},{8,40},{16,48},{24,56},{32,64},{40,72},{48,80},{56,88},{64,... | collective-permute-start | bytes 393224 | tf_op jit(solution)/shard_map/ppermute | solution.py:21
  153.8 6.3 %collective-permute-start.29 = (bf16[512,128]{1,0:T(8,128)(2,1)S(1)}, bf16[512,128]{1,0:T(8,128)(2,1)S(1)}, u32[]{:S(2)}, u32[]{:S(2)}) collective-permute-start(bf16[512,128]{1,0:T(8,128)(2,1)S(1)} %copy-done.2), channel_id=1, source_target_pairs={{0,24},{8,32},{16,40},{24,48},{32,56},{40,64},{48,72},{56,80},{64,... | collective-permute-start | bytes 393224 | tf_op jit(solution)/shard_map/ppermute | solution.py:21
  160.2 5.3 %collective-permute-start.30 = (bf16[512,128]{1,0:T(8,128)(2,1)S(1)}, bf16[512,128]{1,0:T(8,128)(2,1)S(1)}, u32[]{:S(2)}, u32[]{:S(2)}) collective-permute-start(bf16[512,128]{1,0:T(8,128)(2,1)S(1)} %copy-done.2), channel_id=1, source_target_pairs={{0,16},{8,24},{16,32},{24,40},{32,48},{40,56},{48,64},{56,72},{64,... | collective-permute-start | bytes 393224 | tf_op jit(solution)/shard_map/ppermute | solution.py:21
  165.5 1.3 collective-permute-start.31
  167.4 1.7 collective-permute-done.31
  169.2 26.6 %while.59 = (s32[]{:T(128)}, bf16[4,128,512]{2,1,0:T(8,128)(2,1)S(1)}, s32[4]{0:T(128)S(1)}, s32[1,32]{1,0:T(1,128)S(1)}, s32[32,1]{0,1:T(1,128)S(1)}, /*index=5...) while((s32[]{:T(128)}, ...), condition=%wide.region_7.8_spmd, body=%wide.region_1.7_spmd.sunk | while | flops 140009488 | bytes 6364730 | solution.py:112
  171.4 0.9 constant_dynamic-slice_fusion.2
  172.7 2.8 while.60
  172.7 1.4 fusion.36
  178.1 0.9 constant_dynamic-slice_fusion.2
  179.3 2.8 while.60
  179.4 1.4 fusion.36
  184.7 0.9 constant_dynamic-slice_fusion.2
  186.0 2.8 while.60
  186.0 1.4 fusion.36
  191.4 0.9 constant_dynamic-slice_fusion.2
  192.6 2.8 while.60
  192.7 1.4 fusion.36
  196.6 204.7 %all-gather.2.cloned.1.call-done = bf16[512,4096]{1,0:T(8,128)(2,1)} async-done(((bf16[512,512]{1,0:T(8,128)(2,1)}), bf16[512,4096]{1,0:T(8,128)(2,1)}) %all-gather.2.cloned.1.call-update) | async-done | bytes 4194320 | tf_op jit(solution)/shard_map/all_gather | solution.py:115
  401.4 6.6 %convolution_convert_fusion = bf16[512,512]{1,0:T(8,128)(2,1)} fusion(bf16[512,4096]{1,0:T(8,128)(2,1)} %all-gather.2.cloned.1.call-done, bf16[4096,512]{1,0:T(8,128)(2,1)} %param.12), kind=kOutput, calls=%fused_computation.35 | convolution fusion | flops 2147745792 | bytes 8912896 | tf_op jit(solution)/shard_map/dot_general | solution.py:114
  (166 shorter events, 17.1 us)
Async XLA Ops:
  6.5 70.5 %copy-start.1 = (bf16[512,128]{1,0:T(8,128)(2,1)S(1)}, bf16[512,128]{1,0:T(8,128)(2,1)}, u32[]{:S(2)}) copy-start(bf16[512,128]{1,0:T(8,128)(2,1)} %param.10) | copy-start | bytes 393220
  6.5 80.7 %copy-start.2 = (bf16[512,128]{1,0:T(8,128)(2,1)S(1)}, bf16[512,128]{1,0:T(8,128)(2,1)}, u32[]{:S(2)}) copy-start(bf16[512,128]{1,0:T(8,128)(2,1)} %param.11) | copy-start | bytes 393220
  6.5 394.8 %all-gather.2.cloned.1.call-start = ((), (), s32[]{:S(2)}) async-start(), calls=%async_computation | async-start | bytes 4718592 | tf_op jit(solution)/shard_map/all_gather | solution.py:115
  6.5 32.1 %collective-permute-start = (bf16[512,128]{1,0:T(8,128)(2,1)}, bf16[512,128]{1,0:T(8,128)(2,1)S(1)}, u32[]{:S(2)}, u32[]{:S(2)}) collective-permute-start(bf16[512,128]{1,0:T(8,128)(2,1)} %param.10), channel_id=1, source_target_pairs={{0,128},{8,136},{16,144},{24,152},{32,160},{40,168},{48,176},{56,1... | collective-permute-start | bytes 393224 | tf_op jit(solution)/shard_map/ppermute | solution.py:21
  11.7 28.3 %collective-permute-start.1 = (bf16[512,128]{1,0:T(8,128)(2,1)}, bf16[512,128]{1,0:T(8,128)(2,1)S(1)}, u32[]{:S(2)}, u32[]{:S(2)}) collective-permute-start(bf16[512,128]{1,0:T(8,128)(2,1)} %param.10), channel_id=1, source_target_pairs={{0,120},{8,128},{16,136},{24,144},{32,152},{40,160},{48,168},{56,1... | collective-permute-start | bytes 393224 | tf_op jit(solution)/shard_map/ppermute | solution.py:21
  23.4 20.4 %collective-permute-start.2 = (bf16[512,128]{1,0:T(8,128)(2,1)}, bf16[512,128]{1,0:T(8,128)(2,1)S(1)}, u32[]{:S(2)}, u32[]{:S(2)}) collective-permute-start(bf16[512,128]{1,0:T(8,128)(2,1)} %param.10), channel_id=1, source_target_pairs={{0,112},{8,120},{16,128},{24,136},{32,144},{40,152},{48,160},{56,1... | collective-permute-start | bytes 393224 | tf_op jit(solution)/shard_map/ppermute | solution.py:21
  27.9 17.3 %collective-permute-start.3 = (bf16[512,128]{1,0:T(8,128)(2,1)}, bf16[512,128]{1,0:T(8,128)(2,1)S(1)}, u32[]{:S(2)}, u32[]{:S(2)}) collective-permute-start(bf16[512,128]{1,0:T(8,128)(2,1)} %param.10), channel_id=1, source_target_pairs={{0,104},{8,112},{16,120},{24,128},{32,136},{40,144},{48,152},{56,1... | collective-permute-start | bytes 393224 | tf_op jit(solution)/shard_map/ppermute | solution.py:21
  29.2 17.8 %collective-permute-start.4 = (bf16[512,128]{1,0:T(8,128)(2,1)}, bf16[512,128]{1,0:T(8,128)(2,1)S(1)}, u32[]{:S(2)}, u32[]{:S(2)}) collective-permute-start(bf16[512,128]{1,0:T(8,128)(2,1)} %param.10), channel_id=1, source_target_pairs={{0,96},{8,104},{16,112},{24,120},{32,128},{40,136},{48,144},{56,15... | collective-permute-start | bytes 393224 | tf_op jit(solution)/shard_map/ppermute | solution.py:21
  38.7 15.7 %collective-permute-start.5 = (bf16[512,128]{1,0:T(8,128)(2,1)}, bf16[512,128]{1,0:T(8,128)(2,1)S(1)}, u32[]{:S(2)}, u32[]{:S(2)}) collective-permute-start(bf16[512,128]{1,0:T(8,128)(2,1)} %param.10), channel_id=1, source_target_pairs={{0,88},{8,96},{16,104},{24,112},{32,120},{40,128},{48,136},{56,144... | collective-permute-start | bytes 393224 | tf_op jit(solution)/shard_map/ppermute | solution.py:21
  40.0 17.4 %collective-permute-start.6 = (bf16[512,128]{1,0:T(8,128)(2,1)}, bf16[512,128]{1,0:T(8,128)(2,1)S(1)}, u32[]{:S(2)}, u32[]{:S(2)}) collective-permute-start(bf16[512,128]{1,0:T(8,128)(2,1)} %param.10), channel_id=1, source_target_pairs={{0,80},{8,88},{16,96},{24,104},{32,112},{40,120},{48,128},{56,136}... | collective-permute-start | bytes 393224 | tf_op jit(solution)/shard_map/ppermute | solution.py:21
  43.9 20.3 %collective-permute-start.7 = (bf16[512,128]{1,0:T(8,128)(2,1)}, bf16[512,128]{1,0:T(8,128)(2,1)S(1)}, u32[]{:S(2)}, u32[]{:S(2)}) collective-permute-start(bf16[512,128]{1,0:T(8,128)(2,1)} %param.10), channel_id=1, source_target_pairs={{0,72},{8,80},{16,88},{24,96},{32,104},{40,112},{48,120},{56,128},... | collective-permute-start | bytes 393224 | tf_op jit(solution)/shard_map/ppermute | solution.py:21
  45.2 30.0 %collective-permute-start.8 = (bf16[512,128]{1,0:T(8,128)(2,1)}, bf16[512,128]{1,0:T(8,128)(2,1)S(1)}, u32[]{:S(2)}, u32[]{:S(2)}) collective-permute-start(bf16[512,128]{1,0:T(8,128)(2,1)} %param.10), channel_id=1, source_target_pairs={{0,64},{8,72},{16,80},{24,88},{32,96},{40,104},{48,112},{56,120},{... | collective-permute-start | bytes 393224 | tf_op jit(solution)/shard_map/ppermute | solution.py:21
  47.1 30.0 %collective-permute-start.9 = (bf16[512,128]{1,0:T(8,128)(2,1)}, bf16[512,128]{1,0:T(8,128)(2,1)S(1)}, u32[]{:S(2)}, u32[]{:S(2)}) collective-permute-start(bf16[512,128]{1,0:T(8,128)(2,1)} %param.10), channel_id=1, source_target_pairs={{0,56},{8,64},{16,72},{24,80},{32,88},{40,96},{48,104},{56,112},{6... | collective-permute-start | bytes 393224 | tf_op jit(solution)/shard_map/ppermute | solution.py:21
  54.4 29.2 %collective-permute-start.10 = (bf16[512,128]{1,0:T(8,128)(2,1)}, bf16[512,128]{1,0:T(8,128)(2,1)S(1)}, u32[]{:S(2)}, u32[]{:S(2)}) collective-permute-start(bf16[512,128]{1,0:T(8,128)(2,1)} %param.10), channel_id=1, source_target_pairs={{0,48},{8,56},{16,64},{24,72},{32,80},{40,88},{48,96},{56,104},{64... | collective-permute-start | bytes 393224 | tf_op jit(solution)/shard_map/ppermute | solution.py:21
  57.4 29.8 %collective-permute-start.11 = (bf16[512,128]{1,0:T(8,128)(2,1)}, bf16[512,128]{1,0:T(8,128)(2,1)S(1)}, u32[]{:S(2)}, u32[]{:S(2)}) collective-permute-start(bf16[512,128]{1,0:T(8,128)(2,1)} %param.10), channel_id=1, source_target_pairs={{0,40},{8,48},{16,56},{24,64},{32,72},{40,80},{48,88},{56,96},{64,... | collective-permute-start | bytes 393224 | tf_op jit(solution)/shard_map/ppermute | solution.py:21
  64.2 28.2 %collective-permute-start.12 = (bf16[512,128]{1,0:T(8,128)(2,1)}, bf16[512,128]{1,0:T(8,128)(2,1)S(1)}, u32[]{:S(2)}, u32[]{:S(2)}) collective-permute-start(bf16[512,128]{1,0:T(8,128)(2,1)} %param.10), channel_id=1, source_target_pairs={{0,32},{8,40},{16,48},{24,56},{32,64},{40,72},{48,80},{56,88},{64,... | collective-permute-start | bytes 393224 | tf_op jit(solution)/shard_map/ppermute | solution.py:21
  75.2 22.7 %collective-permute-start.13 = (bf16[512,128]{1,0:T(8,128)(2,1)}, bf16[512,128]{1,0:T(8,128)(2,1)S(1)}, u32[]{:S(2)}, u32[]{:S(2)}) collective-permute-start(bf16[512,128]{1,0:T(8,128)(2,1)} %param.10), channel_id=1, source_target_pairs={{0,24},{8,32},{16,40},{24,48},{32,56},{40,64},{48,72},{56,80},{64,... | collective-permute-start | bytes 393224 | tf_op jit(solution)/shard_map/ppermute | solution.py:21
  77.1 26.0 %collective-permute-start.14 = (bf16[512,128]{1,0:T(8,128)(2,1)S(1)}, bf16[512,128]{1,0:T(8,128)(2,1)S(1)}, u32[]{:S(2)}, u32[]{:S(2)}) collective-permute-start(bf16[512,128]{1,0:T(8,128)(2,1)S(1)} %copy-done.1), channel_id=1, source_target_pairs={{0,16},{8,24},{16,32},{24,40},{32,48},{40,56},{48,64},{56,72},{64,... | collective-permute-start | bytes 393224 | tf_op jit(solution)/shard_map/ppermute | solution.py:21
  83.6 26.5 %collective-permute-start.15 = (bf16[512,128]{1,0:T(8,128)(2,1)S(1)}, bf16[512,128]{1,0:T(8,128)(2,1)S(1)}, u32[]{:S(2)}, u32[]{:S(2)}) collective-permute-start(bf16[512,128]{1,0:T(8,128)(2,1)S(1)} %copy-done.1), channel_id=1, source_target_pairs={{0,8},{8,16},{16,24},{24,32},{32,40},{40,48},{48,56},{56,64},{64,7... | collective-permute-start | bytes 393224 | tf_op jit(solution)/shard_map/ppermute | solution.py:21
  87.2 29.9 %collective-permute-start.16 = (bf16[512,128]{1,0:T(8,128)(2,1)S(1)}, bf16[512,128]{1,0:T(8,128)(2,1)S(1)}, u32[]{:S(2)}, u32[]{:S(2)}) collective-permute-start(bf16[512,128]{1,0:T(8,128)(2,1)S(1)} %copy-done.2), channel_id=1, source_target_pairs={{0,128},{8,136},{16,144},{24,152},{32,160},{40,168},{48,176},{56,1... | collective-permute-start | bytes 393224 | tf_op jit(solution)/shard_map/ppermute | solution.py:21
  92.4 26.7 %collective-permute-start.17 = (bf16[512,128]{1,0:T(8,128)(2,1)S(1)}, bf16[512,128]{1,0:T(8,128)(2,1)S(1)}, u32[]{:S(2)}, u32[]{:S(2)}) collective-permute-start(bf16[512,128]{1,0:T(8,128)(2,1)S(1)} %copy-done.2), channel_id=1, source_target_pairs={{0,120},{8,128},{16,136},{24,144},{32,152},{40,160},{48,168},{56,1... | collective-permute-start | bytes 393224 | tf_op jit(solution)/shard_map/ppermute | solution.py:21
  97.9 25.4 %collective-permute-start.18 = (bf16[512,128]{1,0:T(8,128)(2,1)S(1)}, bf16[512,128]{1,0:T(8,128)(2,1)S(1)}, u32[]{:S(2)}, u32[]{:S(2)}) collective-permute-start(bf16[512,128]{1,0:T(8,128)(2,1)S(1)} %copy-done.2), channel_id=1, source_target_pairs={{0,112},{8,120},{16,128},{24,136},{32,144},{40,152},{48,160},{56,1... | collective-permute-start | bytes 393224 | tf_op jit(solution)/shard_map/ppermute | solution.py:21
  103.1 22.1 %collective-permute-start.19 = (bf16[512,128]{1,0:T(8,128)(2,1)S(1)}, bf16[512,128]{1,0:T(8,128)(2,1)S(1)}, u32[]{:S(2)}, u32[]{:S(2)}) collective-permute-start(bf16[512,128]{1,0:T(8,128)(2,1)S(1)} %copy-done.2), channel_id=1, source_target_pairs={{0,104},{8,112},{16,120},{24,128},{32,136},{40,144},{48,152},{56,1... | collective-permute-start | bytes 393224 | tf_op jit(solution)/shard_map/ppermute | solution.py:21
  110.2 19.3 %collective-permute-start.20 = (bf16[512,128]{1,0:T(8,128)(2,1)S(1)}, bf16[512,128]{1,0:T(8,128)(2,1)S(1)}, u32[]{:S(2)}, u32[]{:S(2)}) collective-permute-start(bf16[512,128]{1,0:T(8,128)(2,1)S(1)} %copy-done.2), channel_id=1, source_target_pairs={{0,96},{8,104},{16,112},{24,120},{32,128},{40,136},{48,144},{56,15... | collective-permute-start | bytes 393224 | tf_op jit(solution)/shard_map/ppermute | solution.py:21
  117.1 52.1 %copy-start.3 = (bf16[8704,128]{1,0:T(8,128)(2,1)}, bf16[8704,128]{1,0:T(8,128)(2,1)S(1)}, u32[]{:S(2)}) copy-start(bf16[8704,128]{1,0:T(8,128)(2,1)S(1)} %constant_dynamic-update-slice_fusion.1) | copy-start | bytes 6684676
  117.1 21.9 %collective-permute-start.21 = (bf16[512,128]{1,0:T(8,128)(2,1)S(1)}, bf16[512,128]{1,0:T(8,128)(2,1)S(1)}, u32[]{:S(2)}, u32[]{:S(2)}) collective-permute-start(bf16[512,128]{1,0:T(8,128)(2,1)S(1)} %copy-done.2), channel_id=1, source_target_pairs={{0,88},{8,96},{16,104},{24,112},{32,120},{40,128},{48,136},{56,144... | collective-permute-start | bytes 393224 | tf_op jit(solution)/shard_map/ppermute | solution.py:21
  119.1 21.3 %collective-permute-start.22 = (bf16[512,128]{1,0:T(8,128)(2,1)S(1)}, bf16[512,128]{1,0:T(8,128)(2,1)S(1)}, u32[]{:S(2)}, u32[]{:S(2)}) collective-permute-start(bf16[512,128]{1,0:T(8,128)(2,1)S(1)} %copy-done.2), channel_id=1, source_target_pairs={{0,80},{8,88},{16,96},{24,104},{32,112},{40,120},{48,128},{56,136}... | collective-permute-start | bytes 393224 | tf_op jit(solution)/shard_map/ppermute | solution.py:21
  123.3 23.8 %collective-permute-start.23 = (bf16[512,128]{1,0:T(8,128)(2,1)S(1)}, bf16[512,128]{1,0:T(8,128)(2,1)S(1)}, u32[]{:S(2)}, u32[]{:S(2)}) collective-permute-start(bf16[512,128]{1,0:T(8,128)(2,1)S(1)} %copy-done.2), channel_id=1, source_target_pairs={{0,72},{8,80},{16,88},{24,96},{32,104},{40,112},{48,120},{56,128},... | collective-permute-start | bytes 393224 | tf_op jit(solution)/shard_map/ppermute | solution.py:21
  125.2 28.6 %collective-permute-start.24 = (bf16[512,128]{1,0:T(8,128)(2,1)S(1)}, bf16[512,128]{1,0:T(8,128)(2,1)S(1)}, u32[]{:S(2)}, u32[]{:S(2)}) collective-permute-start(bf16[512,128]{1,0:T(8,128)(2,1)S(1)} %copy-done.2), channel_id=1, source_target_pairs={{0,64},{8,72},{16,80},{24,88},{32,96},{40,104},{48,112},{56,120},{... | collective-permute-start | bytes 393224 | tf_op jit(solution)/shard_map/ppermute | solution.py:21
  129.5 30.7 %collective-permute-start.25 = (bf16[512,128]{1,0:T(8,128)(2,1)S(1)}, bf16[512,128]{1,0:T(8,128)(2,1)S(1)}, u32[]{:S(2)}, u32[]{:S(2)}) collective-permute-start(bf16[512,128]{1,0:T(8,128)(2,1)S(1)} %copy-done.2), channel_id=1, source_target_pairs={{0,56},{8,64},{16,72},{24,80},{32,88},{40,96},{48,104},{56,112},{6... | collective-permute-start | bytes 393224 | tf_op jit(solution)/shard_map/ppermute | solution.py:21
  139.0 26.6 %collective-permute-start.26 = (bf16[512,128]{1,0:T(8,128)(2,1)S(1)}, bf16[512,128]{1,0:T(8,128)(2,1)S(1)}, u32[]{:S(2)}, u32[]{:S(2)}) collective-permute-start(bf16[512,128]{1,0:T(8,128)(2,1)S(1)} %copy-done.2), channel_id=1, source_target_pairs={{0,48},{8,56},{16,64},{24,72},{32,80},{40,88},{48,96},{56,104},{64... | collective-permute-start | bytes 393224 | tf_op jit(solution)/shard_map/ppermute | solution.py:21
  140.4 26.5 %collective-permute-start.27 = (bf16[512,128]{1,0:T(8,128)(2,1)S(1)}, bf16[512,128]{1,0:T(8,128)(2,1)S(1)}, u32[]{:S(2)}, u32[]{:S(2)}) collective-permute-start(bf16[512,128]{1,0:T(8,128)(2,1)S(1)} %copy-done.2), channel_id=1, source_target_pairs={{0,40},{8,48},{16,56},{24,64},{32,72},{40,80},{48,88},{56,96},{64,... | collective-permute-start | bytes 393224 | tf_op jit(solution)/shard_map/ppermute | solution.py:21
  147.1 19.8 %collective-permute-start.28 = (bf16[512,128]{1,0:T(8,128)(2,1)S(1)}, bf16[512,128]{1,0:T(8,128)(2,1)S(1)}, u32[]{:S(2)}, u32[]{:S(2)}) collective-permute-start(bf16[512,128]{1,0:T(8,128)(2,1)S(1)} %copy-done.2), channel_id=1, source_target_pairs={{0,32},{8,40},{16,48},{24,56},{32,64},{40,72},{48,80},{56,88},{64,... | collective-permute-start | bytes 393224 | tf_op jit(solution)/shard_map/ppermute | solution.py:21
  153.8 13.2 %collective-permute-start.29 = (bf16[512,128]{1,0:T(8,128)(2,1)S(1)}, bf16[512,128]{1,0:T(8,128)(2,1)S(1)}, u32[]{:S(2)}, u32[]{:S(2)}) collective-permute-start(bf16[512,128]{1,0:T(8,128)(2,1)S(1)} %copy-done.2), channel_id=1, source_target_pairs={{0,24},{8,32},{16,40},{24,48},{32,56},{40,64},{48,72},{56,80},{64,... | collective-permute-start | bytes 393224 | tf_op jit(solution)/shard_map/ppermute | solution.py:21
  160.2 7.3 %collective-permute-start.30 = (bf16[512,128]{1,0:T(8,128)(2,1)S(1)}, bf16[512,128]{1,0:T(8,128)(2,1)S(1)}, u32[]{:S(2)}, u32[]{:S(2)}) collective-permute-start(bf16[512,128]{1,0:T(8,128)(2,1)S(1)} %copy-done.2), channel_id=1, source_target_pairs={{0,16},{8,24},{16,32},{24,40},{32,48},{40,56},{48,64},{56,72},{64,... | collective-permute-start | bytes 393224 | tf_op jit(solution)/shard_map/ppermute | solution.py:21
  165.5 3.6 collective-permute-start.31
  195.8 0.8 copy-start
Sparse Core Ops, SparseCore 0:
  196.7 204.5 all-gather.1
where the time goes:
time: 417 us; the launch traced here: 415 us
  waiting for transfers between devices  207 us (50%)
  starting transfers between devices  157 us (38%)
  matrix products  15.3 us (4%)
  between operations  14.2 us (3%)
  local copies, waits for them, and re-layouts  10.4 us (2%)
  other arithmetic  6.59 us (2%)
    all_gather x1, waiting for transfers between devices, local(): lax.all_gather(attended, 'head', axis=1, tiled=True)  205 us
    ppermute x32, starting transfers between devices, from_behind(): lax.ppermute(value, axis, [(source, source + steps) for source in range(l...  157 us
  transfers between devices with their start and end apart: 33, of which 3 were waited for; matrix products, arithmetic and copies ran while one was open for 1% of the time, Pallas kernels for 0%

commit v1 on v0

v1 whole, which is shorter than its diff:
```python
import functools
import math

import jax
import jax.numpy as jnp
from jax import lax
from jax.experimental import pallas as pl
from jax.experimental.pallas import tpu as pltpu
from jax.sharding import PartitionSpec as P

HD = 128
GROUP = 4
PIECE = 512
ROW = 8
NEG = -1e30
EXP_SCALE = math.log2(math.e) / math.sqrt(HD)


def query_bounds(place_ref, lens_ref, count):
    first = place_ref[0] * PIECE
    pos = first + lax.broadcasted_iota(jnp.int32, (1, PIECE), 1)

    def step(j, carried):
        at, start, start_first = carried
        start = jnp.where(pos >= at, at, start)
        start_first = jnp.where(first >= at, at, start_first)
        return (at + lens_ref[j], start, start_first)

    zero = jnp.int32(0)
    _, start, start_first = lax.fori_loop(0, count, step, (zero, jnp.zeros_like(pos), zero))
    return first, pos, start, start_first


def attend(q_ref, keys, values, m_ref, l_ref, acc_ref, allowed):
    for h in range(GROUP):
        cols = slice(h * HD, (h + 1) * HD)
        lanes = slice(h * PIECE, (h + 1) * PIECE)
        s = lax.dot_general(
            keys, q_ref[:, cols], (((1,), (1,)), ((), ())), preferred_element_type=jnp.float32
        )
        if allowed is not None:
            s = jnp.where(allowed, s, NEG)
        m_old = m_ref[:, lanes]
        m_new = jnp.maximum(m_old, jnp.max(s, axis=0, keepdims=True))
        p = jnp.exp2((s - m_new) * EXP_SCALE)
        alpha = jnp.exp2((m_old - m_new) * EXP_SCALE)
        m_ref[:, lanes] = m_new
        l_ref[:, lanes] = l_ref[:, lanes] * alpha + jnp.sum(p, axis=0, keepdims=True)
        o = lax.dot_general(
            values, p.astype(jnp.bfloat16), (((0,), (0,)), ((), ())), preferred_element_type=jnp.float32
        )
        acc_ref[:, lanes] = acc_ref[:, lanes] * alpha + o


def diagonal_kernel(place_ref, lens_ref, q_ref, kv_ref, m_ref, l_ref, acc_ref):
    first, pos, start, _ = query_bounds(place_ref, lens_ref, lens_ref.shape[0])
    m_ref[...] = jnp.full_like(m_ref, NEG)
    l_ref[...] = jnp.zeros_like(l_ref)
    acc_ref[...] = jnp.zeros_like(acc_ref)
    key_pos = first + lax.broadcasted_iota(jnp.int32, (PIECE, 1), 0)
    allowed = (key_pos >= start) & (key_pos <= pos)
    attend(q_ref, kv_ref[:, :HD], kv_ref[:, HD:], m_ref, l_ref, acc_ref, allowed)


def row_kernel(back, last, place_ref, lens_ref, q_ref, kv_ref, m_in, l_in, acc_in, *refs):
    if last:
        out_ref, m_ref, l_ref, acc_ref = refs
    else:
        m_ref, l_ref, acc_ref = refs
    first, pos, start, start_first = query_bounds(place_ref, lens_ref, lens_ref.shape[0])
    m_ref[...] = m_in[...]
    l_ref[...] = l_in[...]
    acc_ref[...] = acc_in[...]
    me = lax.rem(place_ref[0], ROW)
    needed = (first - start_first + PIECE - 1) // PIECE
    low = jnp.maximum(1, me + 1 + (back - 1) * ROW)
    high = jnp.minimum(needed, me + back * ROW)

    def step(distance, _):
        piece = me - distance + back * ROW
        rows = pl.ds(pl.multiple_of(piece * PIECE, PIECE), PIECE)
        keys = kv_ref[rows, :HD]
        values = kv_ref[rows, HD:]
        key_first = first - distance * PIECE
        whole = (key_first >= start_first) & (start_first + 0 >= start_last)

        @pl.when(whole)
        def _():
            attend(q_ref, keys, values, m_ref, l_ref, acc_ref, None)

        @pl.when(jnp.logical_not(whole))
        def _():
            key_pos = key_first + lax.broadcasted_iota(jnp.int32, (PIECE, 1), 0)
            attend(q_ref, keys, values, m_ref, l_ref, acc_ref, key_pos >= start)

        return 0

    start_last = jnp.max(start)
    lax.fori_loop(low, high + 1, step, 0)
    if last:
        for h in range(GROUP):
            lanes = slice(h * PIECE, (h + 1) * PIECE)
            o = acc_ref[:, lanes] / l_ref[:, lanes]
            out_ref[:, h * HD : (h + 1) * HD] = o.T.astype(jnp.bfloat16)


def state_shapes():
    lanes = GROUP * PIECE
    return [
        jax.ShapeDtypeStruct((1, lanes), jnp.float32),
        jax.ShapeDtypeStruct((1, lanes), jnp.float32),
        jax.ShapeDtypeStruct((HD, lanes), jnp.float32),
    ]


SMEM = pl.BlockSpec(memory_space=pltpu.SMEM)
VMEM = pl.BlockSpec(memory_space=pltpu.VMEM)


def attention_cost(pieces):
    flops = 4 * pieces * PIECE * GROUP * PIECE * HD
    return pl.CostEstimate(flops=flops, bytes_accessed=4 << 20, transcendentals=pieces * GROUP * PIECE * PIECE)


def diagonal(place, lens, q, kv):
    return pl.pallas_call(
        diagonal_kernel,
        out_shape=state_shapes(),
        in_specs=[SMEM, SMEM, VMEM, VMEM],
        out_specs=[VMEM] * 3,
        cost_estimate=attention_cost(1),
        name="diagonal",
    )(place, lens, q, kv)


def row(back, last, place, lens, q, kv, state):
    lanes = GROUP * PIECE
    if last:
        out_shape = jax.ShapeDtypeStruct((PIECE, GROUP * HD), jnp.bfloat16)
        out_specs = VMEM
        scratch = [
            pltpu.VMEM((1, lanes), jnp.float32),
            pltpu.VMEM((1, lanes), jnp.float32),
            pltpu.VMEM((HD, lanes), jnp.float32),
        ]
    else:
        out_shape = state_shapes()
        out_specs = [VMEM] * 3
        scratch = []
    return pl.pallas_call(
        functools.partial(row_kernel, back, last),
        out_shape=out_shape,
        in_specs=[SMEM, SMEM] + [VMEM] * 5,
        out_specs=out_specs,
        scratch_shapes=scratch,
        cost_estimate=attention_cost(ROW),
        name="row%d" % back,
    )(place, lens, q, kv, *state)


def local(query_rows, key_rows, value_rows, out_weight, doc_lengths):
    count = lax.axis_size("tok")
    place = lax.axis_index("tok").astype(jnp.int32).reshape(1)
    rows = [list(range(r, r + ROW)) for r in range(0, count, ROW)]
    kv = jnp.concatenate([key_rows, value_rows], axis=1)
    behind1 = lax.ppermute(kv, "tok", [(i, i + ROW) for i in range(count - ROW)])
    behind2 = lax.ppermute(kv, "tok", [(i, i + 2 * ROW) for i in range(count - 2 * ROW)])

    def gather(x):
        return lax.all_gather(x, "tok", axis=0, tiled=True, axis_index_groups=rows)

    state = diagonal(place, doc_lengths, query_rows, kv)
    state = row(0, False, place, doc_lengths, query_rows, gather(kv), state)
    state = row(1, False, place, doc_lengths, query_rows, gather(behind1), state)
    attended = row(2, True, place, doc_lengths, query_rows, gather(behind2), state)
    mixed = jnp.dot(
        lax.all_gather(attended, "head", axis=1, tiled=True),
        out_weight,
        preferred_element_type=jnp.float32,
    )
    return mixed.astype(jnp.bfloat16)


def solution(mesh):
    return jax.shard_map(
        local,
        mesh=mesh,
        in_specs=(P("tok", "head"), P("tok", "head"), P("tok", "head"), P(None, "head"), P()),
        out_specs=P("tok", "head"),
        check_vma=False,
    )
```

time: 417 us -> 213 us (0.51); the launches traced: 415 us -> 216 us
  starting transfers between devices: 157 us -> 10.9 us
  waiting for transfers between devices: 207 us -> 166 us
  Pallas kernels: 0 us -> 15.2 us
  matrix products: 15.3 us -> 6.59 us
  other arithmetic: 6.59 us -> 0 us
  local copies, waits for them, and re-layouts: 10.4 us -> 3.99 us
    all_gather x1, waiting for transfers between devices: 205 us -> 55.4 us  [local(): lax.all_gather(attended, 'head', axis=1, tiled=True)]
    ppermute x32 -> x2, starting transfers between devices: 157 us -> 10.7 us  [the longest x1 6.7 us: local(): lax.ppermute(kv, 'tok', [(i, i + 2 * ROW) for i in range(count - 2 * ROW)])]
    all_gather x0 -> x3, waiting for transfers between devices: none -> 102 us  [gather(): return lax.all_gather(x, 'tok', axis=0, tiled=True, axis_index_groups=rows)]
    pallas_call x0 -> x4, Pallas kernels: none -> 15.2 us  [the longest x3 10.4 us: row(): pl.pallas_call(functools.partial(row_kernel, back, last), out_shape=out_s...]
    dot_general x8 -> x0, matrix products: 8.76 us -> none  [the longest x4 5.56 us: attend_block(): jnp.einsum('crd,kcd->crk', queries, key_block, preferred_element_type=jnp...]
    dynamic_slice x12 -> x0, local copies, waits for them, and re-layouts: 6.8 us -> none  [local(): lax.map(run_slot, (query_rows.reshape(per_device, TILE, q_width), tile_st...]
    ppermute x32 -> x2, waiting for transfers between devices: 2.18 us -> 8.06 us  [the longest x1 4.46 us: local(): lax.ppermute(kv, 'tok', [(i, i + 2 * ROW) for i in range(count - 2 * ROW)])]
  transfers between devices with their start and end apart: 33 -> 6, of which waited for: 3 -> 6; matrix products, arithmetic and copies ran while one was open for 1% -> 0% of each run, Pallas kernels for 0% -> 5%
where the time goes in v1:
time: 213 us; the launch traced here: 216 us
  waiting for transfers between devices  166 us (78%)
  Pallas kernels  15.2 us (7%)
  between operations  13.2 us (6%)
  starting transfers between devices  10.9 us (5%)
  matrix products  6.59 us (3%)
  local copies, waits for them, and re-layouts  3.99 us (2%)
    all_gather x3, waiting for transfers between devices, gather(): return lax.all_gather(x, 'tok', axis=0, tiled=True, axis_index_groups=rows)  102 us
    all_gather x1, waiting for transfers between devices, local(): lax.all_gather(attended, 'head', axis=1, tiled=True)  55.4 us
    pallas_call x3, Pallas kernels, row(): pl.pallas_call(functools.partial(row_kernel, back, last), out_shape=out_s...  10.4 us
    ppermute x1, starting transfers between devices, local(): lax.ppermute(kv, 'tok', [(i, i + 2 * ROW) for i in range(count - 2 * ROW)])  6.7 us
    dot_general x1, matrix products, local(): jnp.dot(lax.all_gather(attended, 'head', axis=1, tiled=True), out_weight,...  6.59 us
    pallas_call x1, Pallas kernels, diagonal(): pl.pallas_call(diagonal_kernel, out_shape=state_shapes(), in_specs=[SMEM,...  4.78 us
    ppermute x1, waiting for transfers between devices, local(): lax.ppermute(kv, 'tok', [(i, i + 2 * ROW) for i in range(count - 2 * ROW)])  4.46 us
  transfers between devices with their start and end apart: 6, of which 6 were waited for; matrix products, arithmetic and copies ran while one was open for 0% of the time, Pallas kernels for 5%

profile of v1, /device:TPU:1, one launch (start us, length us, event | category | flops | bytes accessed | tf_op | source)
XLA Modules:
  0.0 215.7 jit_solution(12113764232788396584)
XLA Ops:
  6.5 0.0 all-gather.9.cloned.1.call-start
  6.5 0.9 constant_dynamic-update-slice_fusion.1
  7.5 0.9 constant_dynamic-update-slice_fusion.kv_ref
  8.4 0.0 copy-start
  8.4 0.7 copy-done
  9.1 0.0 all-gather.9.cloned.1.call-update
  9.1 0.0 all-gather.7.cloned.1.call-start
  9.2 4.0 %collective-permute-start.1 = (bf16[512,256]{1,0:T(8,128)(2,1)}, bf16[512,256]{1,0:T(8,128)(2,1)S(1)}, u32[]{:S(2)}, u32[]{:S(2)}) collective-permute-start(bf16[512,256]{1,0:T(8,128)(2,1)} %copy-done), channel_id=1, source_target_pairs={{0,64},{8,72},{16,80},{24,88},{32,96},{40,104},{48,112},{56,120},{... | collective-permute-start | bytes 786440 | tf_op jit(solution)/shard_map/ppermute | solution.py:166
  13.2 3.6 %collective-permute-done.1 = bf16[512,256]{1,0:T(8,128)(2,1)S(1)} collective-permute-done((bf16[512,256]{1,0:T(8,128)(2,1)}, bf16[512,256]{1,0:T(8,128)(2,1)S(1)}, u32[]{:S(2)}, u32[]{:S(2)}) %collective-permute-start.1) | collective-permute-done | bytes 262176 | tf_op jit(solution)/shard_map/ppermute | solution.py:166
  16.8 0.0 copy-start.1
  16.8 0.7 copy-done.1
  17.5 0.0 all-gather.7.cloned.1.call-update
  17.6 0.0 all-gather.5.cloned.1.call-start
  17.6 6.7 %collective-permute-start = (bf16[512,256]{1,0:T(8,128)(2,1)}, bf16[512,256]{1,0:T(8,128)(2,1)S(1)}, u32[]{:S(2)}, u32[]{:S(2)}) collective-permute-start(bf16[512,256]{1,0:T(8,128)(2,1)} %copy-done), channel_id=1, source_target_pairs={{0,128},{8,136},{16,144},{24,152},{32,160},{40,168},{48,176},{56,1... | collective-permute-start | bytes 786440 | tf_op jit(solution)/shard_map/ppermute | solution.py:167
  24.3 4.5 %collective-permute-done = bf16[512,256]{1,0:T(8,128)(2,1)S(1)} collective-permute-done((bf16[512,256]{1,0:T(8,128)(2,1)}, bf16[512,256]{1,0:T(8,128)(2,1)S(1)}, u32[]{:S(2)}, u32[]{:S(2)}) %collective-permute-start) | collective-permute-done | bytes 262176 | tf_op jit(solution)/shard_map/ppermute | solution.py:167
  28.8 0.0 copy-start.2
  28.8 0.7 copy-done.2
  29.5 0.0 all-gather.5.cloned.1.call-update
  29.5 0.0 all-gather.11.cloned.1.call-start
  29.6 4.8 %diagonal.1 = (f32[1,2048]{1,0:T(1,128)}, f32[1,2048]{1,0:T(1,128)}, f32[128,2048]{1,0:T(8,128)}) custom-call(s32[1]{0:T(128)} %bitcast.place_ref, s32[32]{0:T(128)} %lens_ref.7, bf16[512,512]{1,0:T(8,128)(2,1)} %q_ref.7, bf16[512,256]{1,0:T(8,128)(2,1)} %copy-done), custom_call_target="tpu_custom_call" | custom-call | flops 536870912 | bytes 4194304 | tf_op jit(solution)/shard_map/diagonal/pallas_call | solution.py:126
  34.4 20.4 %all-gather.9.cloned.1.call-done.kv_ref = bf16[4096,256]{1,0:T(8,128)(2,1)} async-done(((bf16[512,256]{1,0:T(8,128)(2,1)}), bf16[4096,256]{1,0:T(8,128)(2,1)}) %all-gather.9.cloned.1.call-update) | async-done | bytes 2097168 | tf_op jit(solution)/shard_map/all_gather | solution.py:170
  54.8 3.5 %row0.1 = (f32[1,2048]{1,0:T(1,128)}, f32[1,2048]{1,0:T(1,128)}, f32[128,2048]{1,0:T(8,128)}) custom-call(s32[1]{0:T(128)} %bitcast.place_ref, s32[32]{0:T(128)} %lens_ref.7, bf16[512,512]{1,0:T(8,128)(2,1)} %q_ref.7, bf16[4096,256]{1,0:T(8,128)(2,1)} %all-gather.9.cloned.1.call-done.kv_ref, f32[1,2048]{1,0:T(1,128)} %get-tuple-element.14.m_in, ...), custom_call_target="tpu_custom_call" | custom-call | flops 4294967296 | bytes 4194304 | tf_op jit(solution)/shard_map/row0/pallas_call | solution.py:150
  58.3 40.9 %all-gather.7.cloned.1.call-done.kv_ref = bf16[4096,256]{1,0:T(8,128)(2,1)} async-done(((bf16[512,256]{1,0:T(8,128)(2,1)}), bf16[4096,256]{1,0:T(8,128)(2,1)}) %all-gather.7.cloned.1.call-update) | async-done | bytes 2097168 | tf_op jit(solution)/shard_map/all_gather | solution.py:170
  99.2 3.4 %row1.1 = (f32[1,2048]{1,0:T(1,128)}, f32[1,2048]{1,0:T(1,128)}, f32[128,2048]{1,0:T(8,128)}) custom-call(s32[1]{0:T(128)} %bitcast.place_ref, s32[32]{0:T(128)} %lens_ref.7, bf16[512,512]{1,0:T(8,128)(2,1)} %q_ref.7, bf16[4096,256]{1,0:T(8,128)(2,1)} %all-gather.7.cloned.1.call-done.kv_ref, f32[1,2048]{1,0:T(1,128)} %get-tuple-element.17.m_in, ...), custom_call_target="tpu_custom_call" | custom-call | flops 4294967296 | bytes 4194304 | tf_op jit(solution)/shard_map/row1/pallas_call | solution.py:150
  102.6 40.9 %all-gather.5.cloned.1.call-done.kv_ref = bf16[4096,256]{1,0:T(8,128)(2,1)} async-done(((bf16[512,256]{1,0:T(8,128)(2,1)}), bf16[4096,256]{1,0:T(8,128)(2,1)}) %all-gather.5.cloned.1.call-update) | async-done | bytes 2097168 | tf_op jit(solution)/shard_map/all_gather | solution.py:170
  143.6 3.5 %row2.1 = bf16[512,512]{1,0:T(8,128)(2,1)} custom-call(s32[1]{0:T(128)} %bitcast.place_ref, s32[32]{0:T(128)} %lens_ref.7, bf16[512,512]{1,0:T(8,128)(2,1)} %q_ref.7, bf16[4096,256]{1,0:T(8,128)(2,1)} %all-gather.5.cloned.1.call-done.kv_ref, f32[1,2048]{1,0:T(1,128)} %get-tuple-element.20.m_in, f32[1,2048]{1,0:T(1,128)} %get-tuple-element.21.l_in, ...), custom_call_target="tpu_custom_call" | custom-call | flops 4294967296 | bytes 4194304 | tf_op jit(solution)/shard_map/row2/pallas_call | solution.py:150
  147.1 0.0 all-gather.11.cloned.1.call-update
  147.1 55.4 %all-gather.11.cloned.1.call-done = bf16[512,4096]{1,0:T(8,128)(2,1)} async-done(((bf16[512,512]{1,0:T(8,128)(2,1)}), bf16[512,4096]{1,0:T(8,128)(2,1)}) %all-gather.11.cloned.1.call-update) | async-done | bytes 4194320 | tf_op jit(solution)/shard_map/all_gather | solution.py:177
  202.5 6.6 %convolution_convert_fusion = bf16[512,512]{1,0:T(8,128)(2,1)} fusion(bf16[512,4096]{1,0:T(8,128)(2,1)} %all-gather.11.cloned.1.call-done, bf16[4096,512]{1,0:T(8,128)(2,1)} %param.8), kind=kOutput, calls=%fused_computation | convolution fusion | flops 2147745792 | bytes 8912896 | tf_op jit(solution)/shard_map/dot_general | solution.py:176
Async XLA Ops:
  6.5 48.3 %all-gather.9.cloned.1.call-start = ((), (), s32[]{:S(2)}) async-start(), calls=%async_computation.2 | async-start | bytes 2359296 | tf_op jit(solution)/shard_map/all_gather | solution.py:170
  8.4 0.7 copy-start
  9.1 90.0 %all-gather.7.cloned.1.call-start = ((), (), s32[]{:S(2)}) async-start(), calls=%async_computation.1 | async-start | bytes 2359296 | tf_op jit(solution)/shard_map/all_gather | solution.py:170
  9.2 7.6 %collective-permute-start.1 = (bf16[512,256]{1,0:T(8,128)(2,1)}, bf16[512,256]{1,0:T(8,128)(2,1)S(1)}, u32[]{:S(2)}, u32[]{:S(2)}) collective-permute-start(bf16[512,256]{1,0:T(8,128)(2,1)} %copy-done), channel_id=1, source_target_pairs={{0,64},{8,72},{16,80},{24,88},{32,96},{40,104},{48,112},{56,120},{... | collective-permute-start | bytes 786440 | tf_op jit(solution)/shard_map/ppermute | solution.py:166
  16.8 0.7 copy-start.1
  17.6 126.0 %all-gather.5.cloned.1.call-start = ((), (), s32[]{:S(2)}) async-start(), calls=%async_computation | async-start | bytes 2359296 | tf_op jit(solution)/shard_map/all_gather | solution.py:170
  17.6 11.2 %collective-permute-start = (bf16[512,256]{1,0:T(8,128)(2,1)}, bf16[512,256]{1,0:T(8,128)(2,1)S(1)}, u32[]{:S(2)}, u32[]{:S(2)}) collective-permute-start(bf16[512,256]{1,0:T(8,128)(2,1)} %copy-done), channel_id=1, source_target_pairs={{0,128},{8,136},{16,144},{24,152},{32,160},{40,168},{48,176},{56,1... | collective-permute-start | bytes 786440 | tf_op jit(solution)/shard_map/ppermute | solution.py:167
  28.8 0.7 copy-start.2
  29.5 173.0 %all-gather.11.cloned.1.call-start = ((), (), s32[]{:S(2)}) async-start(), calls=%async_computation.3 | async-start | bytes 4718592 | tf_op jit(solution)/shard_map/all_gather | solution.py:177
Sparse Core Ops, SparseCore 0:
  9.4 45.3 all-gather.8
  56.9 42.2 all-gather.6
  101.3 42.2 all-gather.4
  147.2 55.2 all-gather.10

commit v2 on v1

v2 whole, which is shorter than its diff:
```python
import functools
import math

import jax
import jax.numpy as jnp
from jax import lax
from jax.experimental import pallas as pl
from jax.experimental.pallas import tpu as pltpu
from jax.sharding import PartitionSpec as P

HD = 128
GROUP = 4
PIECE = 512
ROW = 8
NEG = -1e30
EXP_SCALE = math.log2(math.e) / math.sqrt(HD)
LANES = ((1,), (1,)), ((), ())
PLAIN = ((1,), (0,)), ((), ())


def query_bounds(place_ref, lens_ref):
    first = place_ref[0] * PIECE
    pos = first + lax.broadcasted_iota(jnp.int32, (1, PIECE), 1)

    def step(j, carried):
        at, start, start_first, start_last = carried
        start = jnp.where(pos >= at, at, start)
        start_first = jnp.where(first >= at, at, start_first)
        start_last = jnp.where(first + PIECE - 1 >= at, at, start_last)
        return (at + lens_ref[j], start, start_first, start_last)

    zero = jnp.int32(0)
    carried = (zero, jnp.zeros_like(pos), zero, zero)
    _, start, start_first, start_last = lax.fori_loop(0, lens_ref.shape[0], step, carried)
    return first, pos, start, start_first, start_last


def scores(q, keys):
    return lax.dot_general(keys, q, LANES, preferred_element_type=jnp.float32)


def absorb(s, values_t, head, state):
    m_ref, l_ref, acc_ref = state
    m_old = m_ref[head]
    m_new = jnp.maximum(m_old, jnp.max(s, axis=0, keepdims=True))
    p = jnp.exp2((s - m_new) * EXP_SCALE)
    alpha = jnp.exp2((m_old - m_new) * EXP_SCALE)
    m_ref[head] = m_new
    l_ref[head] = l_ref[head] * alpha + jnp.sum(p, axis=0, keepdims=True)
    o = lax.dot_general(values_t, p.astype(jnp.bfloat16), PLAIN, preferred_element_type=jnp.float32)
    acc_ref[head] = acc_ref[head] * alpha + o


def values_of(kv):
    return jnp.concatenate([kv[b * HD : (b + 1) * HD, HD:] for b in range(PIECE // HD)], axis=1)


def pack_kernel(k_ref, v_ref, kv_ref):
    kv_ref[0, :, :HD] = k_ref[...]
    for b in range(PIECE // HD):
        rows = slice(b * HD, (b + 1) * HD)
        kv_ref[0, rows, HD:] = v_ref[rows, :].T


def diagonal_kernel(place_ref, lens_ref, q_ref, kv_ref, m_ref, l_ref, acc_ref, qt_ref):
    first, pos, start, _, _ = query_bounds(place_ref, lens_ref)
    m_ref[...] = jnp.full_like(m_ref, NEG)
    l_ref[...] = jnp.zeros_like(l_ref)
    acc_ref[...] = jnp.zeros_like(acc_ref)
    key_pos = first + lax.broadcasted_iota(jnp.int32, (PIECE, 1), 0)
    allowed = (key_pos >= start) & (key_pos <= pos)
    kv = kv_ref[0]
    for h in range(GROUP):
        qt_ref[h] = q_ref[:, h * HD : (h + 1) * HD]
        s = jnp.where(allowed, scores(qt_ref[h], kv[:, :HD]), NEG)
        absorb(s, values_of(kv), h, (m_ref, l_ref, acc_ref))


def pieces_kernel(distance, slots, place_ref, lens_ref, q_ref, kv_ref, m_in, l_in, acc_in, m_ref, l_ref, acc_ref, s_even, s_odd):
    del m_in, l_in, acc_in
    first, _, start, start_first, start_last = query_bounds(place_ref, lens_ref)
    state = (m_ref, l_ref, acc_ref)
    buffers = (s_even, s_odd)

    def piece(slot, _):
        key_first = first - (distance + slot * ROW) * PIECE
        needed = key_first + PIECE > start_first
        whole = key_first >= start_last

        @pl.when(needed & whole)
        def _():
            s_even[...] = scores(q_ref[0], kv_ref[slot, :, :HD])
            for h in range(GROUP):
                if h + 1 < GROUP:
                    buffers[(h + 1) % 2][...] = scores(q_ref[h + 1], kv_ref[slot, :, :HD])
                absorb(buffers[h % 2][...], values_of(kv_ref[slot]), h, state)

        @pl.when(needed & jnp.logical_not(whole))
        def _():
            key_pos = key_first + lax.broadcasted_iota(jnp.int32, (PIECE, 1), 0)

            def one(h, _):
                s = jnp.where(key_pos >= start, scores(q_ref[h], kv_ref[slot, :, :HD]), NEG)
                absorb(s, values_of(kv_ref[slot]), h, state)
                return 0

            lax.fori_loop(0, GROUP, one, 0)

        return 0

    lax.fori_loop(0, slots, piece, 0)


def finish_kernel(l_ref, acc_ref, out_ref):
    for h in range(GROUP):
        o = acc_ref[h] / l_ref[h]
        out_ref[:, h * HD : (h + 1) * HD] = o.T.astype(jnp.bfloat16)


STATE = [
    jax.ShapeDtypeStruct((GROUP, 1, PIECE), jnp.float32),
    jax.ShapeDtypeStruct((GROUP, 1, PIECE), jnp.float32),
    jax.ShapeDtypeStruct((GROUP, HD, PIECE), jnp.float32),
]
SMEM = pl.BlockSpec(memory_space=pltpu.SMEM)
VMEM = pl.BlockSpec(memory_space=pltpu.VMEM)


def cost(pieces):
    flops = 4 * pieces * PIECE * GROUP * PIECE * HD
    return pl.CostEstimate(flops=flops, bytes_accessed=1 << 20, transcendentals=pieces * GROUP * PIECE * PIECE)


def params(mib):
    return pltpu.CompilerParams(vmem_limit_bytes=mib << 20)


def pack(k, v):
    return pl.pallas_call(
        pack_kernel,
        out_shape=jax.ShapeDtypeStruct((1, PIECE, 2 * HD), jnp.bfloat16),
        in_specs=[VMEM, VMEM],
        out_specs=VMEM,
        compiler_params=params(8),
        name="pack",
    )(k, v)


def diagonal(place, lens, q, kv):
    *state, qt = pl.pallas_call(
        diagonal_kernel,
        out_shape=STATE + [jax.ShapeDtypeStruct((GROUP, PIECE, HD), jnp.bfloat16)],
        in_specs=[SMEM, SMEM, VMEM, VMEM],
        out_specs=[VMEM] * 4,
        cost_estimate=cost(1),
        compiler_params=params(24),
        name="diagonal",
    )(place, lens, q, kv)
    return state, qt


def pieces(distance, place, lens, q, kv, state):
    slots = kv.shape[0]
    return pl.pallas_call(
        functools.partial(pieces_kernel, distance, slots),
        out_shape=STATE,
        in_specs=[SMEM, SMEM] + [VMEM] * 5,
        out_specs=[VMEM] * 3,
        scratch_shapes=[pltpu.VMEM((PIECE, PIECE), jnp.float32)] * 2,
        input_output_aliases={4: 0, 5: 1, 6: 2},
        cost_estimate=cost(slots),
        compiler_params=params(24),
        name="pieces%d" % distance,
    )(place, lens, q, kv, *state)


def finish(state):
    return pl.pallas_call(
        finish_kernel,
        out_shape=jax.ShapeDtypeStruct((PIECE, GROUP * HD), jnp.bfloat16),
        in_specs=[VMEM, VMEM],
        out_specs=VMEM,
        compiler_params=params(8),
        name="finish",
    )(state[1], state[2])


def shift(value, steps):
    count = lax.axis_size("tok")
    return lax.ppermute(value, "tok", [(i, (i + steps) % count) for i in range(count)])


def local(query_rows, key_rows, value_rows, out_weight, doc_lengths):
    place = lax.axis_index("tok").astype(jnp.int32).reshape(1)
    kv = pack(key_rows, value_rows)
    back8 = shift(kv, ROW)
    up = [shift(jnp.concatenate([kv, back8]), 1)]
    back16 = shift(back8, ROW)
    down = [shift(jnp.concatenate([back8, back16]), -1)]
    up.append(shift(up[-1], 1))
    down.append(shift(down[-1], -1))
    up.append(shift(up[-1], 1))
    down.append(shift(down[-1], -1))
    up.append(shift(up[-1], 1))

    state, q = diagonal(place, doc_lengths, query_rows, kv)
    order = [(8, back8), (16, back16), (1, up[0]), (7, down[0]), (2, up[1])]
    order += [(6, down[1]), (3, up[2]), (5, down[2]), (4, up[3])]
    for distance, arrived in order:
        state = pieces(distance, place, doc_lengths, q, arrived, state)
    mixed = jnp.dot(
        lax.all_gather(finish(state), "head", axis=1, tiled=True),
        out_weight,
        preferred_element_type=jnp.float32,
    )
    return mixed.astype(jnp.bfloat16)


def solution(mesh):
    return jax.shard_map(
        local,
        mesh=mesh,
        in_specs=(P("tok", "head"), P("tok", "head"), P("tok", "head"), P(None, "head"), P()),
        out_specs=P("tok", "head"),
        check_vma=False,
    )
```

time: 213 us -> 178 us (0.84); the launches traced: 216 us -> 178 us
  waiting for transfers between devices: 166 us -> 102 us
  starting transfers between devices: 10.9 us -> 40.7 us
  Pallas kernels: 15.2 us -> 12 us
    all_gather x4 -> x1, waiting for transfers between devices: 158 us -> 67.4 us  [local(): lax.all_gather(finish(state), 'head', axis=1, tiled=True)]
    ppermute x2 -> x9, starting transfers between devices: 10.7 us -> 40.7 us  [shift(): lax.ppermute(value, 'tok', [(i, (i + steps) % count) for i in range(count)])]
    ppermute x2 -> x9, waiting for transfers between devices: 8.06 us -> 34.2 us  [shift(): lax.ppermute(value, 'tok', [(i, (i + steps) % count) for i in range(count)])]
    pallas_call x4 -> x12, Pallas kernels: 15.2 us -> 12 us  [the longest x9 7.66 us: pieces(): pl.pallas_call(functools.partial(pieces_kernel, distance, slots), out_sha...]
  transfers between devices with their start and end apart: 6 -> 10, of which waited for: 6 -> 6; matrix products, arithmetic and copies ran while one was open for 0% -> 0% of each run, Pallas kernels for 5% -> 6%
where the time goes in v2:
time: 178 us
  waiting for transfers between devices  102 us (57%)
  starting transfers between devices  40.7 us (23%)
  between operations  13.6 us (8%)
  Pallas kernels  12 us (7%)
  matrix products  6.59 us (4%)
  local copies, waits for them, and re-layouts  3.5 us (2%)
    all_gather x1, waiting for transfers between devices, local(): lax.all_gather(finish(state), 'head', axis=1, tiled=True)  67.4 us
    ppermute x9, starting transfers between devices, shift(): lax.ppermute(value, 'tok', [(i, (i + steps) % count) for i in range(count)])  40.7 us
    ppermute x9, waiting for transfers between devices, shift(): lax.ppermute(value, 'tok', [(i, (i + steps) % count) for i in range(count)])  34.2 us
    pallas_call x9, Pallas kernels, pieces(): pl.pallas_call(functools.partial(pieces_kernel, distance, slots), out_sha...  7.66 us
    dot_general x1, matrix products, local(): jnp.dot(lax.all_gather(finish(state), 'head', axis=1, tiled=True), out_we...  6.59 us
  transfers between devices with their start and end apart: 10, of which 6 were waited for; matrix products, arithmetic and copies ran while one was open for 0% of the time, Pallas kernels for 6%

profile of v2, /device:TPU:1, one launch (start us, length us, event | category | flops | bytes accessed | tf_op | source)
XLA Modules:
  0.0 178.1 jit_solution(4968480913684494917)
XLA Ops:
  6.5 0.0 all-gather.2.cloned.1.call-start
  6.5 0.0 copy-start
  6.5 0.9 copy-done
  7.4 0.0 copy-start.1
  7.4 0.9 copy-done.1
  8.3 0.0 copy-start.4
  8.3 0.1 pack.1.kv_ref
  8.4 4.0 %collective-permute-start = (bf16[1,512,256]{2,1,0:T(8,128)(2,1)S(1)}, bf16[1,512,256]{2,1,0:T(8,128)(2,1)S(1)}, u32[]{:S(2)}, u32[]{:S(2)}) collective-permute-start(bf16[1,512,256]{2,1,0:T(8,128)(2,1)S(1)} %pack.1.kv_ref), channel_id=1, source_target_pairs={{0,64},{8,72},{16,80},{24,88},{32,96},{40,104},{48,112},{56,120},{... | collective-permute-start | bytes 786440 | tf_op jit(solution)/shard_map/ppermute | solution.py:190
  12.5 5.6 %collective-permute-done.kv_ref = bf16[1,512,256]{2,1,0:T(8,128)(2,1)S(1)} collective-permute-done((bf16[1,512,256]{2,1,0:T(8,128)(2,1)S(1)}, bf16[1,512,256]{2,1,0:T(8,128)(2,1)S(1)}, u32[]{:S(2)}, u32[]{:S(2)}) %collective-permute-start) | collective-permute-done | bytes 262176 | tf_op jit(solution)/shard_map/ppermute | solution.py:190
  18.1 2.5 %collective-permute-start.5 = (bf16[1,512,256]{2,1,0:T(8,128)(2,1)S(1)}, bf16[1,512,256]{2,1,0:T(8,128)(2,1)S(1)}, u32[]{:S(2)}, u32[]{:S(2)}) collective-permute-start(bf16[1,512,256]{2,1,0:T(8,128)(2,1)S(1)} %collective-permute-done.kv_ref), channel_id=1, source_target_pairs={{0,64},{8,72},{16,80},{24,88},{32,96},{40,104},{48,112},{56,120},{... | collective-permute-start | bytes 786440 | tf_op jit(solution)/shard_map/ppermute | solution.py:190
  20.6 6.5 %collective-permute-done.5.kv_ref = bf16[1,512,256]{2,1,0:T(8,128)(2,1)S(1)} collective-permute-done((bf16[1,512,256]{2,1,0:T(8,128)(2,1)S(1)}, bf16[1,512,256]{2,1,0:T(8,128)(2,1)S(1)}, u32[]{:S(2)}, u32[]{:S(2)}) %collective-permute-start.5) | collective-permute-done | bytes 262176 | tf_op jit(solution)/shard_map/ppermute | solution.py:190
  27.2 0.1 pad_maximum_fusion.1
  27.3 6.9 %collective-permute-start.1 = (bf16[2,512,256]{2,1,0:T(8,128)(2,1)S(1)}, bf16[2,512,256]{2,1,0:T(8,128)(2,1)S(1)}, u32[]{:S(2)}, u32[]{:S(2)}) collective-permute-start(bf16[2,512,256]{2,1,0:T(8,128)(2,1)S(1)} %get-tuple-element.66), channel_id=1, source_target_pairs={{0,8},{8,16},{16,24},{24,32},{32,40},{40,48},{48,56},{56,64},{64,7... | collective-permute-start | bytes 1572872 | tf_op jit(solution)/shard_map/ppermute | solution.py:190
  34.2 8.0 %collective-permute-start.6 = (bf16[2,512,256]{2,1,0:T(8,128)(2,1)S(1)}, bf16[2,512,256]{2,1,0:T(8,128)(2,1)S(1)}, u32[]{:S(2)}, u32[]{:S(2)}) collective-permute-start(bf16[2,512,256]{2,1,0:T(8,128)(2,1)S(1)} %get-tuple-element.65), channel_id=1, source_target_pairs={{0,504},{8,0},{16,8},{24,16},{32,24},{40,32},{48,40},{56,48},{64,5... | collective-permute-start | bytes 1572872 | tf_op jit(solution)/shard_map/ppermute | solution.py:190
  42.2 8.0 %collective-permute-done.1.kv_ref = bf16[2,512,256]{2,1,0:T(8,128)(2,1)S(1)} collective-permute-done((bf16[2,512,256]{2,1,0:T(8,128)(2,1)S(1)}, bf16[2,512,256]{2,1,0:T(8,128)(2,1)S(1)}, u32[]{:S(2)}, u32[]{:S(2)}) %collective-permute-start.1) | collective-permute-done | bytes 524320 | tf_op jit(solution)/shard_map/ppermute | solution.py:190
  50.1 1.9 %collective-permute-start.2 = (bf16[2,512,256]{2,1,0:T(8,128)(2,1)S(1)}, bf16[2,512,256]{2,1,0:T(8,128)(2,1)S(1)}, u32[]{:S(2)}, u32[]{:S(2)}) collective-permute-start(bf16[2,512,256]{2,1,0:T(8,128)(2,1)S(1)} %collective-permute-done.1.kv_ref), channel_id=1, source_target_pairs={{0,8},{8,16},{16,24},{24,32},{32,40},{40,48},{48,56},{56,64},{64,7... | collective-permute-start | bytes 1572872 | tf_op jit(solution)/shard_map/ppermute | solution.py:190
  52.1 0.0 collective-permute-done.6.kv_ref
  52.1 6.7 %collective-permute-start.7 = (bf16[2,512,256]{2,1,0:T(8,128)(2,1)S(1)}, bf16[2,512,256]{2,1,0:T(8,128)(2,1)S(1)}, u32[]{:S(2)}, u32[]{:S(2)}) collective-permute-start(bf16[2,512,256]{2,1,0:T(8,128)(2,1)S(1)} %collective-permute-done.6.kv_ref), channel_id=1, source_target_pairs={{0,504},{8,0},{16,8},{24,16},{32,24},{40,32},{48,40},{56,48},{64,5... | collective-permute-start | bytes 1572872 | tf_op jit(solution)/shard_map/ppermute | solution.py:190
  58.8 7.1 %collective-permute-done.2.kv_ref = bf16[2,512,256]{2,1,0:T(8,128)(2,1)S(1)} collective-permute-done((bf16[2,512,256]{2,1,0:T(8,128)(2,1)S(1)}, bf16[2,512,256]{2,1,0:T(8,128)(2,1)S(1)}, u32[]{:S(2)}, u32[]{:S(2)}) %collective-permute-start.2) | collective-permute-done | bytes 524320 | tf_op jit(solution)/shard_map/ppermute | solution.py:190
  65.9 1.9 %collective-permute-start.3 = (bf16[2,512,256]{2,1,0:T(8,128)(2,1)S(1)}, bf16[2,512,256]{2,1,0:T(8,128)(2,1)S(1)}, u32[]{:S(2)}, u32[]{:S(2)}) collective-permute-start(bf16[2,512,256]{2,1,0:T(8,128)(2,1)S(1)} %collective-permute-done.2.kv_ref), channel_id=1, source_target_pairs={{0,8},{8,16},{16,24},{24,32},{32,40},{40,48},{48,56},{56,64},{64,7... | collective-permute-start | bytes 1572872 | tf_op jit(solution)/shard_map/ppermute | solution.py:190
  67.8 0.0 copy-start.2
  67.8 1.0 copy-done.2
  68.8 0.0 copy-start.3
  68.8 0.7 copy-done.3
  69.5 3.3 %diagonal.1 = (f32[4,1,512]{2,1,0:T(1,128)S(1)}, f32[4,1,512]{2,1,0:T(1,128)S(1)}, f32[4,128,512]{2,1,0:T(8,128)S(1)}, bf16[4,512,128]{2,1,0:T(8,128)(2,1)S(1)}) custom-call(s32[1]{0:T(128)} %bitcast.place_ref, s32[32]{0:T(128)S(1)} %copy-done.3, bf16[512,512]{1,0:T(8,128)(2,1)S(1)} %copy-done.2, bf16[1,512,256]{2,1,0:T(8,128)(2,1)S(1)} %pack.1.kv_ref), custom_call_target="tpu_custom_call" | custom-call | flops 536870912 | bytes 1048576 | tf_op jit(solution)/shard_map/diagonal/pallas_call | solution.py:150
  72.8 0.8 pieces8.1
  73.6 0.0 collective-permute-done.7.kv_ref
  73.6 6.7 %collective-permute-start.8 = (bf16[2,512,256]{2,1,0:T(8,128)(2,1)S(1)}, bf16[2,512,256]{2,1,0:T(8,128)(2,1)S(1)}, u32[]{:S(2)}, u32[]{:S(2)}) collective-permute-start(bf16[2,512,256]{2,1,0:T(8,128)(2,1)S(1)} %collective-permute-done.7.kv_ref), channel_id=1, source_target_pairs={{0,504},{8,0},{16,8},{24,16},{32,24},{40,32},{48,40},{56,48},{64,5... | collective-permute-start | bytes 1572872 | tf_op jit(solution)/shard_map/ppermute | solution.py:190
  80.3 0.0 copy-done.4
  80.3 0.8 pieces16.1
  81.1 0.0 collective-permute-done.3.kv_ref
  81.1 2.1 %collective-permute-start.4 = (bf16[2,512,256]{2,1,0:T(8,128)(2,1)S(1)}, bf16[2,512,256]{2,1,0:T(8,128)(2,1)S(1)}, u32[]{:S(2)}, u32[]{:S(2)}) collective-permute-start(bf16[2,512,256]{2,1,0:T(8,128)(2,1)S(1)} %collective-permute-done.3.kv_ref), channel_id=1, source_target_pairs={{0,8},{8,16},{16,24},{24,32},{32,40},{40,48},{48,56},{56,64},{64,7... | collective-permute-start | bytes 1572872 | tf_op jit(solution)/shard_map/ppermute | solution.py:190
  83.2 0.8 pieces1.1
  84.1 0.8 pieces7.1
  84.9 0.8 pieces2.1
  85.7 0.8 pieces6.1
  86.6 0.8 pieces3.1
  87.4 0.0 collective-permute-done.8.kv_ref
  87.4 1.1 pieces5.1
  88.5 6.9 %collective-permute-done.4.kv_ref = bf16[2,512,256]{2,1,0:T(8,128)(2,1)S(1)} collective-permute-done((bf16[2,512,256]{2,1,0:T(8,128)(2,1)S(1)}, bf16[2,512,256]{2,1,0:T(8,128)(2,1)S(1)}, u32[]{:S(2)}, u32[]{:S(2)}) %collective-permute-start.4) | collective-permute-done | bytes 524320 | tf_op jit(solution)/shard_map/ppermute | solution.py:190
  95.4 0.8 pieces4.1
  96.3 1.0 finish.1
  97.3 0.0 all-gather.2.cloned.1.call-update
  97.3 67.4 %all-gather.2.cloned.1.call-done = bf16[512,4096]{1,0:T(8,128)(2,1)} async-done(((bf16[512,512]{1,0:T(8,128)(2,1)}), bf16[512,4096]{1,0:T(8,128)(2,1)}) %all-gather.2.cloned.1.call-update) | async-done | bytes 4194320 | tf_op jit(solution)/shard_map/all_gather | solution.py:212
  164.7 6.6 %convolution_convert_fusion = bf16[512,512]{1,0:T(8,128)(2,1)} fusion(bf16[512,4096]{1,0:T(8,128)(2,1)} %all-gather.2.cloned.1.call-done, bf16[4096,512]{1,0:T(8,128)(2,1)} %param.8), kind=kOutput, calls=%fused_computation | convolution fusion | flops 2147745792 | bytes 8912896 | tf_op jit(solution)/shard_map/dot_general | solution.py:211
Async XLA Ops:
  6.5 158.2 %all-gather.2.cloned.1.call-start = ((), (), s32[]{:S(2)}) async-start(), calls=%async_computation | async-start | bytes 4718592 | tf_op jit(solution)/shard_map/all_gather | solution.py:212
  6.5 0.9 copy-start
  7.4 0.9 copy-start.1
  8.3 71.9 %copy-start.4 = (s32[32]{0:T(128)S(1)}, s32[32]{0:T(128)}, u32[]{:S(2)}) copy-start(s32[32]{0:T(128)} %lens_ref.19) | copy-start | bytes 388
  8.4 9.7 %collective-permute-start = (bf16[1,512,256]{2,1,0:T(8,128)(2,1)S(1)}, bf16[1,512,256]{2,1,0:T(8,128)(2,1)S(1)}, u32[]{:S(2)}, u32[]{:S(2)}) collective-permute-start(bf16[1,512,256]{2,1,0:T(8,128)(2,1)S(1)} %pack.1.kv_ref), channel_id=1, source_target_pairs={{0,64},{8,72},{16,80},{24,88},{32,96},{40,104},{48,112},{56,120},{... | collective-permute-start | bytes 786440 | tf_op jit(solution)/shard_map/ppermute | solution.py:190
  18.1 9.1 %collective-permute-start.5 = (bf16[1,512,256]{2,1,0:T(8,128)(2,1)S(1)}, bf16[1,512,256]{2,1,0:T(8,128)(2,1)S(1)}, u32[]{:S(2)}, u32[]{:S(2)}) collective-permute-start(bf16[1,512,256]{2,1,0:T(8,128)(2,1)S(1)} %collective-permute-done.kv_ref), channel_id=1, source_target_pairs={{0,64},{8,72},{16,80},{24,88},{32,96},{40,104},{48,112},{56,120},{... | collective-permute-start | bytes 786440 | tf_op jit(solution)/shard_map/ppermute | solution.py:190
  27.3 22.9 %collective-permute-start.1 = (bf16[2,512,256]{2,1,0:T(8,128)(2,1)S(1)}, bf16[2,512,256]{2,1,0:T(8,128)(2,1)S(1)}, u32[]{:S(2)}, u32[]{:S(2)}) collective-permute-start(bf16[2,512,256]{2,1,0:T(8,128)(2,1)S(1)} %get-tuple-element.66), channel_id=1, source_target_pairs={{0,8},{8,16},{16,24},{24,32},{32,40},{40,48},{48,56},{56,64},{64,7... | collective-permute-start | bytes 1572872 | tf_op jit(solution)/shard_map/ppermute | solution.py:190
  34.2 17.9 %collective-permute-start.6 = (bf16[2,512,256]{2,1,0:T(8,128)(2,1)S(1)}, bf16[2,512,256]{2,1,0:T(8,128)(2,1)S(1)}, u32[]{:S(2)}, u32[]{:S(2)}) collective-permute-start(bf16[2,512,256]{2,1,0:T(8,128)(2,1)S(1)} %get-tuple-element.65), channel_id=1, source_target_pairs={{0,504},{8,0},{16,8},{24,16},{32,24},{40,32},{48,40},{56,48},{64,5... | collective-permute-start | bytes 1572872 | tf_op jit(solution)/shard_map/ppermute | solution.py:190
  50.1 15.7 %collective-permute-start.2 = (bf16[2,512,256]{2,1,0:T(8,128)(2,1)S(1)}, bf16[2,512,256]{2,1,0:T(8,128)(2,1)S(1)}, u32[]{:S(2)}, u32[]{:S(2)}) collective-permute-start(bf16[2,512,256]{2,1,0:T(8,128)(2,1)S(1)} %collective-permute-done.1.kv_ref), channel_id=1, source_target_pairs={{0,8},{8,16},{16,24},{24,32},{32,40},{40,48},{48,56},{56,64},{64,7... | collective-permute-start | bytes 1572872 | tf_op jit(solution)/shard_map/ppermute | solution.py:190
  52.1 21.5 %collective-permute-start.7 = (bf16[2,512,256]{2,1,0:T(8,128)(2,1)S(1)}, bf16[2,512,256]{2,1,0:T(8,128)(2,1)S(1)}, u32[]{:S(2)}, u32[]{:S(2)}) collective-permute-start(bf16[2,512,256]{2,1,0:T(8,128)(2,1)S(1)} %collective-permute-done.6.kv_ref), channel_id=1, source_target_pairs={{0,504},{8,0},{16,8},{24,16},{32,24},{40,32},{48,40},{56,48},{64,5... | collective-permute-start | bytes 1572872 | tf_op jit(solution)/shard_map/ppermute | solution.py:190
  65.9 15.2 %collective-permute-start.3 = (bf16[2,512,256]{2,1,0:T(8,128)(2,1)S(1)}, bf16[2,512,256]{2,1,0:T(8,128)(2,1)S(1)}, u32[]{:S(2)}, u32[]{:S(2)}) collective-permute-start(bf16[2,512,256]{2,1,0:T(8,128)(2,1)S(1)} %collective-permute-done.2.kv_ref), channel_id=1, source_target_pairs={{0,8},{8,16},{16,24},{24,32},{32,40},{40,48},{48,56},{56,64},{64,7... | collective-permute-start | bytes 1572872 | tf_op jit(solution)/shard_map/ppermute | solution.py:190
  67.8 1.0 copy-start.2
  68.8 0.7 copy-start.3
  73.6 13.8 %collective-permute-start.8 = (bf16[2,512,256]{2,1,0:T(8,128)(2,1)S(1)}, bf16[2,512,256]{2,1,0:T(8,128)(2,1)S(1)}, u32[]{:S(2)}, u32[]{:S(2)}) collective-permute-start(bf16[2,512,256]{2,1,0:T(8,128)(2,1)S(1)} %collective-permute-done.7.kv_ref), channel_id=1, source_target_pairs={{0,504},{8,0},{16,8},{24,16},{32,24},{40,32},{48,40},{56,48},{64,5... | collective-permute-start | bytes 1572872 | tf_op jit(solution)/shard_map/ppermute | solution.py:190
  81.1 14.3 %collective-permute-start.4 = (bf16[2,512,256]{2,1,0:T(8,128)(2,1)S(1)}, bf16[2,512,256]{2,1,0:T(8,128)(2,1)S(1)}, u32[]{:S(2)}, u32[]{:S(2)}) collective-permute-start(bf16[2,512,256]{2,1,0:T(8,128)(2,1)S(1)} %collective-permute-done.3.kv_ref), channel_id=1, source_target_pairs={{0,8},{8,16},{16,24},{24,32},{32,40},{40,48},{48,56},{56,64},{64,7... | collective-permute-start | bytes 1572872 | tf_op jit(solution)/shard_map/ppermute | solution.py:190
Sparse Core Ops, SparseCore 0:
  97.4 67.2 all-gather.1
